TPU v7x, 128 devices: a whole 4x4x4 slice. The times are simulated.
128 devices in a mesh: seq: 8 (over y, core), tile: 16 (over z, x).
Axes of the slice: x: 4, y: 4, z: 4, core: 2. Of those that a mesh axis runs over, the one named last changes fastest.
Arguments:
- latents: bfloat16 [16384, 128], P(('seq', 'tile')), may hold values from -6 to 6
- grid_slot: int32 [16384], P(('seq', 'tile')), may hold values from 0 to 16383, as said below
- w_in: bfloat16 [432, 384], replicated, may hold values from -0.3125 to 0.3125
- b_in: float32 [384], replicated, may hold values from -3 to 3
- gain_in: float32 [384], replicated, may hold values from 0.1 to 1.9
- w_up: bfloat16 [3456, 192], replicated, may hold values from -0.109375 to 0.109375
- b_up: float32 [192], replicated, may hold values from -3 to 3
- gain_res: float32 [192], replicated, may hold values from 0.1 to 1.9
- w_res: bfloat16 [5184, 192], replicated, may hold values from -0.078125 to 0.078125
- b_res: float32 [192], replicated, may hold values from -3 to 3
Outputs:
- decoded: bfloat16 [16, 128, 49152], P(None, 'tile', 'seq')
Inputs may be any that keep to these rules, and one draw needn't show every extreme that they name: grid_slot is a permutation of 0 to 16383. Row r of the sequence lies on device r // 128 and grid row p on device p // 128 (devices in the order seq then tile). The rows of one device go to exactly 64 receiving devices, exactly 2 rows to each, so every device receives 128 rows; the receivers of device d are d + k modulo 128 for a set of offsets k common to all devices, which includes 128 / 2.
All inputs are finite; a program needn't handle non-finite values.
Results may differ from a plain program's by a relative error of at most 0.0058.
Values may be sent and summed in bfloat16 or wider, within the bound.
No kernel may reach another device: no remote copies, remote signals or barrier semaphores. Data moves between devices by JAX's collectives and lax.ppermute only.
A program may use at most 192 MiB of HBM per device.

v0:
```python
import jax
import jax.numpy as jnp
from jax import lax
from jax.sharding import PartitionSpec as P

LAT = 16
C1 = 384
C2 = 192
FS = 2
TH = 4
W = 128


def extended_2(block, sides, width):
    for axis, dim in sides:
        count = lax.axis_size(axis)
        forward = [(i, i + 1) for i in range(count - 1)]
        backward = [(target, source) for source, target in forward]
        low = lax.ppermute(
            lax.slice_in_dim(block, block.shape[dim] - width, None, axis=dim), axis, forward
        )
        high = lax.ppermute(lax.slice_in_dim(block, 0, width, axis=dim), axis, backward)
        block = jnp.concatenate([low, block, high], axis=dim)
    return block


def from_behind(x, axis, by):
    length = lax.axis_size(axis)
    pairs = [(i, i + by) for i in range(length) if 0 <= i + by < length]
    return lax.ppermute(x, axis, pairs)


def causal_taps(padded, weight, bias):
    frames = padded.shape[0] - 2
    height = padded.shape[1] - 2
    breadth = padded.shape[2] - 2
    channels = padded.shape[3]
    running = jnp.zeros((frames * height * breadth, weight.shape[1]), jnp.float32)
    for time_off in range(3):
        for row_off in range(3):
            window = jnp.concatenate(
                [
                    padded[
                        time_off : time_off + frames,
                        row_off : row_off + height,
                        col_off : col_off + breadth,
                    ]
                    for col_off in range(3)
                ],
                axis=-1,
            )
            start = (time_off * 3 + row_off) * 3 * channels
            running = running + jnp.dot(
                window.reshape(-1, 3 * channels),
                weight[start : start + 3 * channels],
                preferred_element_type=jnp.float32,
            )
    return (running + bias).reshape(frames, height, breadth, weight.shape[1])


def upsample_conv(extended, weight, bias):
    doubled = jnp.repeat(jnp.repeat(extended, 2, axis=1), 2, axis=2)[:, 1:-1, 1:-1]
    frames = doubled.shape[0]
    height = doubled.shape[1] - 2
    breadth = doubled.shape[2] - 2
    channels = doubled.shape[3]
    running = jnp.zeros((frames * height * breadth, weight.shape[1]), jnp.float32)
    for row_off in range(3):
        window = jnp.concatenate(
            [
                doubled[:, row_off : row_off + height, col_off : col_off + breadth]
                for col_off in range(3)
            ],
            axis=-1,
        )
        start = row_off * 3 * channels
        running = running + jnp.dot(
            window.reshape(-1, 3 * channels),
            weight[start : start + 3 * channels],
            preferred_element_type=jnp.float32,
        )
    return (running + bias).astype(jnp.bfloat16).reshape(frames, height, breadth, weight.shape[1])


def normed_silu(values, gain):
    scaled = values * lax.rsqrt(jnp.mean(values * values, axis=-1, keepdims=True) + 1e-06) * gain
    return jax.nn.silu(scaled).astype(jnp.bfloat16)


def local(latents, grid_slot, w_in, b_in, gain_in, w_up, b_up, gain_res, w_res, b_res):
    seq_count = lax.axis_size("seq")
    tile_count = lax.axis_size("tile")
    device_count = seq_count * tile_count
    row_count = latents.shape[0]
    row_width = latents.shape[1]
    slot_cap = 2 * row_count // device_count
    target = grid_slot // row_count
    local_row = grid_slot % row_count
    one_hot = (target[:, None] == jnp.arange(device_count, dtype=jnp.int32)[None, :]).astype(
        jnp.int32
    )
    rank_in = jnp.sum((jnp.cumsum(one_hot, axis=0) - 1) * one_hot, axis=1)
    send_slot = target * slot_cap + rank_in
    outbox = (
        jnp.zeros((device_count * slot_cap, row_width), latents.dtype).at[send_slot].set(latents)
    )
    labels = jnp.full((device_count * slot_cap,), row_count, jnp.int32).at[send_slot].set(local_row)
    inbox_rows, inbox_labels = (
        lax.all_to_all(
            outbox.reshape(device_count, slot_cap, row_width),
            ("seq", "tile"),
            split_axis=0,
            concat_axis=0,
            tiled=True,
        ),
        lax.all_to_all(
            labels.reshape(device_count, slot_cap),
            ("seq", "tile"),
            split_axis=0,
            concat_axis=0,
            tiled=True,
        ),
    )
    grid_rows = (
        jnp.zeros((row_count, row_width), jnp.bfloat16)
        .at[inbox_labels.reshape(-1)]
        .set(inbox_rows.reshape(-1, row_width), mode="drop")
    )
    grid_latent = grid_rows.reshape(FS, TH, W * LAT)
    extended = extended_2(grid_latent, (("tile", 1),), 1)
    before = from_behind(extended, "seq", 1)
    window_in = jnp.concatenate([before, extended], axis=0).reshape(FS + 2, TH + 2, W, LAT)
    window_in = jnp.pad(window_in, ((0, 0), (0, 0), (1, 1), (0, 0)))
    first_conv = causal_taps(window_in, w_in, b_in)
    first_act = normed_silu(first_conv, gain_in)
    act_ext = extended_2(first_act.reshape(FS, TH, W * C1), (("tile", 1),), 1)
    act_ext = jnp.pad(act_ext.reshape(FS, TH + 2, W, C1), ((0, 0), (0, 0), (1, 1), (0, 0)))
    section_out = upsample_conv(act_ext, w_up, b_up)
    upsampled = lax.all_to_all(
        section_out.reshape(FS, 2 * TH, 2 * W * C2), "seq", split_axis=2, concat_axis=0, tiled=True
    )
    upsampled = upsampled.reshape(FS * seq_count, 2 * TH, 2 * W // seq_count, C2)
    res_act = normed_silu(upsampled.astype(jnp.float32), gain_res)
    res_ext = extended_2(res_act, (("seq", 2), ("tile", 1)), 1)
    res_ext = jnp.pad(res_ext, ((2, 0), (0, 0), (0, 0), (0, 0)))
    res_conv = causal_taps(res_ext, w_res, b_res)
    decoded = (upsampled.astype(jnp.float32) + res_conv).astype(jnp.bfloat16)
    return decoded.reshape(decoded.shape[0], 2 * TH, -1)


def solution(mesh):
    return jax.shard_map(
        local,
        mesh=mesh,
        in_specs=(
            P(("seq", "tile"), None),
            P(("seq", "tile")),
            P(),
            P(),
            P(),
            P(),
            P(),
            P(),
            P(),
            P(),
        ),
        out_specs=P(None, "tile", "seq"),
        check_vma=False,
    )
```

profile of v0, /device:TPU:7, one launch (start us, length us, event | category | flops | bytes accessed | tf_op | source)
XLA Modules:
  0.0 614.1 jit_solution(8333284277565260925)
XLA Ops:
  2.9 10.8 %all-to-all-start = ((s32[128,1,2]{2,1,0:T(1,128)}), s32[128,1,2]{2,1,0:T(1,128)S(1)}, u32[]{:S(2)}, u32[]{:S(2)}) async-start(s32[128,1,2]{2,1,0:T(1,128)} %bitcast), calls=%async_computation | async-start | bytes 131072 | tf_op jit(solution)/shard_map/all_to_all | solution.py:116
  15.4 6.2 %all-to-all-done = s32[128,1,2]{2,1,0:T(1,128)S(1)} async-done(((s32[128,1,2]{2,1,0:T(1,128)}), s32[128,1,2]{2,1,0:T(1,128)S(1)}, u32[]{:S(2)}, u32[]{:S(2)}) %all-to-all-start) | async-done | bytes 1056 | tf_op jit(solution)/shard_map/all_to_all | solution.py:116
  21.6 6.1 all-to-all-start.1
  29.1 6.5 %all-to-all-done.1 = bf16[128,2,128]{2,1,0:T(2,128)(2,1)S(1)} async-done(((bf16[128,2,128]{2,1,0:T(2,128)(2,1)}), bf16[128,2,128]{2,1,0:T(2,128)(2,1)S(1)}, u32[]{:S(2)}, u32[]{:S(2)}) %all-to-all-start.1) | async-done | bytes 65568 | tf_op jit(solution)/shard_map/all_to_all | solution.py:109
  36.9 2.4 collective-permute-start.1
  39.3 5.0 collective-permute-start
  45.2 4.3 collective-permute-start.2
  62.3 2.5 pad_maximum_fusion.22
  66.0 2.4 fusion.39
  71.8 2.6 pad_maximum_fusion.20
  79.0 2.4 fusion.45
  87.5 4.8 multiply_reduce_fusion.1
  95.8 4.5 fusion.17
  102.5 6.5 %collective-permute-start.3 = (bf16[2,1,49152]{2,0,1:T(2,128)(2,1)S(1)}, bf16[2,1,49152]{2,0,1:T(2,128)(2,1)S(1)}, u32[]{:S(2)}, u32[]{:S(2)}) collective-permute-start(bf16[2,1,49152]{2,0,1:T(2,128)(2,1)S(1)} %get-tuple-element.44), channel_id=1, source_target_pairs={{0,1},{1,2},{2,3},{3,4},{4,5},{5,6},{6,7},{7,8},{8,9},{9,10},{10,1... | collective-permute-start | bytes 589832 | tf_op jit(solution)/shard_map/ppermute | solution.py:19
  116.5 2.7 broadcast_in_dim.14
  119.1 20.7 %fusion.57 = (bf16[2,8,256,384]{3,0,2,1:T(2,128)(2,1)S(1)}, bf16[2,8,256,384]{3,0,2,1:T(2,128)(2,1)}, bf16[2,8,256,384]{3,0,2,1:T(2,128)(2,1)}, bf16[2,8,256,384...) fusion(bf16[2,12,260,384]{3,0,2,1:T(2,128)(2,1)S(1)} %bitcast.103), kind=kLoop, calls=%fused_computation.140 | loop fusion | bytes 56623104 | tf_op jit(solution)/shard_map/slice | solution.py:71
  139.9 30.7 %pad_maximum_fusion = bf16[2,8,256,1152]{3,0,2,1:T(2,128)(2,1)} fusion(bf16[2,8,256,384]{3,0,2,1:T(2,128)(2,1)S(1)} %get-tuple-element.11, bf16[2,8,256,384]{3,0,2,1:T(2,128)(2,1)S(1)} %get-tuple-element.12, bf16[2,8,256,384]{3,0,2,1:T(2,128)(2,1)S(1)} %get-tuple-element.13), kind=kLoop, calls=%fused_computation.3 | loop fusion | flops 28311552 | bytes 18874368 | tf_op jit(solution)/shard_map/concatenate | solution.py:69
  170.6 9.1 %copy.133 = bf16[2,8,256,1152]{3,2,1,0:T(8,128)(2,1)} copy(bf16[2,8,256,1152]{3,0,2,1:T(2,128)(2,1)} %pad_maximum_fusion) | data formatting | bytes 18874368 | tf_op jit(solution)/shard_map/concatenate | solution.py:69
  179.7 13.1 %pad_maximum_fusion.1 = bf16[2,8,256,1152]{3,0,2,1:T(2,128)(2,1)} fusion(bf16[2,8,256,384]{3,0,2,1:T(2,128)(2,1)} %get-tuple-element.8, bf16[2,8,256,384]{3,0,2,1:T(2,128)(2,1)} %get-tuple-element.9, bf16[2,8,256,384]{3,0,2,1:T(2,128)(2,1)} %get-tuple-element.10), kind=kLoop, calls=%fused_computation.4 | loop fusion | flops 28311552 | bytes 18874368 | tf_op jit(solution)/shard_map/concatenate | solution.py:69
  192.7 9.1 %copy.134 = bf16[2,8,256,1152]{3,2,1,0:T(8,128)(2,1)} copy(bf16[2,8,256,1152]{3,0,2,1:T(2,128)(2,1)} %pad_maximum_fusion.1) | data formatting | bytes 18874368 | tf_op jit(solution)/shard_map/concatenate | solution.py:69
  201.8 31.2 %pad_maximum_fusion.2 = bf16[2,8,256,1152]{3,0,2,1:T(2,128)(2,1)} fusion(bf16[2,8,256,384]{3,0,2,1:T(2,128)(2,1)} %get-tuple-element.6, bf16[2,8,256,384]{3,0,2,1:T(2,128)(2,1)} %get-tuple-element.7, bf16[2,8,256,384]{3,0,2,1:T(2,128)(2,1)S(1)} %get-tuple-element.5), kind=kLoop, calls=%fused_computation.5 | loop fusion | flops 28311552 | bytes 18874368 | tf_op jit(solution)/shard_map/concatenate | solution.py:69
  233.1 9.2 %copy.135 = bf16[2,8,256,1152]{3,2,1,0:T(8,128)(2,1)} copy(bf16[2,8,256,1152]{3,0,2,1:T(2,128)(2,1)} %pad_maximum_fusion.2) | data formatting | bytes 18874368 | tf_op jit(solution)/shard_map/concatenate | solution.py:69
  242.3 7.1 %fusion.20 = f32[4096,192]{0,1:T(8,128)S(1)} fusion(bf16[4096,1152]{1,0:T(8,128)(2,1)} %bitcast.119, bf16[3456,192]{0,1:T(8,128)(2,1)S(1)} %copy-done.18), kind=kOutput, calls=%fused_computation.58 | convolution fusion | flops 1811939328 | bytes 13025280 | tf_op jit(solution)/shard_map/dot_general | solution.py:77
  249.4 7.1 %convolution_add_fusion.8 = f32[4096,192]{0,1:T(8,128)S(1)} fusion(f32[4096,192]{0,1:T(8,128)S(1)} %fusion.20, bf16[4096,1152]{1,0:T(8,128)(2,1)} %bitcast.106, bf16[3456,192]{0,1:T(8,128)(2,1)S(1)} %copy-done.18), kind=kOutput, calls=%fused_computation.35 | convolution fusion | flops 1812725760 | bytes 16171008 | tf_op jit(solution)/shard_map/dot_general | solution.py:77
  256.5 4.4 fusion.10
  260.9 3.1 copy.136
  264.1 3.2 reshape_reshape.3
  267.3 44.1 %copy.137 = bf16[2,8,49152]{1,0,2:T(2,128)(2,1)} copy(bf16[2,8,49152]{2,1,0:T(8,128)(2,1)} %reshape_reshape.3) | data formatting | bytes 3145728 | tf_op jit(solution)/shard_map/reshape;reshape | solution.py:140
  311.4 29.3 %reshape.257 = bf16[8,2,49152]{2,1,0:T(2,128)(2,1)S(1)} reshape(bf16[49152,2,8]{2,1,0:T(2,128)(2,1)} %bitcast.104) | data formatting | bytes 3145728
  340.7 24.8 %all_to_all.23 = bf16[8,2,49152]{2,1,0:T(2,128)(2,1)S(1)} all-to-all(bf16[8,2,49152]{2,1,0:T(2,128)(2,1)S(1)} %reshape.257), channel_id=1, replica_groups=mesh['seq'=8,'tile'=16] {'seq'}, dimensions={0} | all-to-all | bytes 3145728 | tf_op jit(solution)/shard_map/all_to_all | solution.py:139
  365.5 31.8 %reshape.258 = bf16[49152,2,8]{2,1,0:T(2,128)(2,1)} reshape(bf16[8,2,49152]{2,1,0:T(2,128)(2,1)S(1)} %all_to_all.23) | data formatting | bytes 3145728
  397.3 45.4 %copy.138 = bf16[2,8,49152]{2,1,0:T(8,128)(2,1)S(1)} copy(bf16[2,8,49152]{1,0,2:T(2,128)(2,1)} %bitcast.105) | data formatting | bytes 3145728 | tf_op jit(solution)/shard_map/all_to_all | solution.py:139
  445.4 3.3 reshape.212
  448.7 3.0 multiply_reduce_fusion
  453.7 2.9 collective-permute-start.6
  456.6 2.6 collective-permute-start.5
  461.5 6.2 %collective-permute-start.7 = (bf16[16,1,34,192]{3,2,1,0:T(8,128)(2,1)S(1)}, bf16[16,1,34,192]{3,2,1,0:T(8,128)(2,1)S(1)}, u32[]{:S(2)}, u32[]{:S(2)}) collective-permute-start(bf16[16,1,34,192]{3,2,1,0:T(8,128)(2,1)S(1)} %get-tuple-element.40), channel_id=1, source_target_pairs={{0,1},{1,2},{2,3},{3,4},{4,5},{5,6},{6,7},{7,8},{8,9},{9,10},{10,1... | collective-permute-start | bytes 626696 | tf_op jit(solution)/shard_map/ppermute | solution.py:19
  469.7 6.1 fusion.5
  475.8 5.0 collective-permute-done.8
  480.8 4.9 maximum_maximum_fusion
  485.7 4.2 fusion.60
  489.9 3.7 fusion.12
  493.6 14.8 %fusion.58 = (bf16[16,8,32,192]{3,2,1,0:T(8,128)(2,1)}, bf16[16,8,32,192]{3,2,1,0:T(8,128)(2,1)}, bf16[16,8,32,192]{3,2,1,0:T(8,128)(2,1)}, bf16[16,8,32,192]{3,...) fusion(bf16[18,10,34,192]{3,2,1,0:T(8,128)(2,1)S(1)} %fusion.12), kind=kLoop, calls=%fused_computation.141 | loop fusion | bytes 56623104 | tf_op jit(solution)/shard_map/slice | solution.py:43
  508.4 7.3 %pad_maximum_fusion.12 = bf16[16,8,32,576]{3,2,1,0:T(8,128)(2,1)} fusion(bf16[16,8,32,192]{3,2,1,0:T(8,128)(2,1)} %get-tuple-element.36, bf16[16,8,32,192]{3,2,1,0:T(8,128)(2,1)} %get-tuple-element.37, bf16[16,8,32,192]{3,2,1,0:T(8,128)(2,1)} %get-tuple-element.35), kind=kLoop, calls=%fused_computation.23 | loop fusion | flops 14155776 | bytes 9437184 | tf_op jit(solution)/shard_map/concatenate | solution.py:41
  515.7 6.2 %fusion.22 = f32[4096,192]{0,1:T(8,128)} fusion(bf16[4096,576]{1,0:T(8,128)(2,1)} %bitcast.114, bf16[5184,192]{0,1:T(8,128)(2,1)} %param.18), kind=kOutput, calls=%fused_computation.72 | convolution fusion | flops 905969664 | bytes 8634368 | tf_op jit(solution)/shard_map/dot_general | solution.py:53
  521.9 6.1 pad_maximum_fusion.5
  528.0 6.1 fusion.31
  534.2 4.3 fusion.59
  538.4 4.5 pad_maximum_fusion.6
  542.9 6.0 convolution_add_fusion.6
  548.9 4.5 pad_maximum_fusion.7
  553.3 5.8 convolution_add_fusion.5
  559.1 4.5 pad_maximum_fusion.8
  563.6 5.8 convolution_add_fusion.4
  569.3 4.5 pad_maximum_fusion.9
  573.8 5.8 convolution_add_fusion.3
  579.6 4.6 pad_maximum_fusion.10
  584.2 5.8 convolution_add_fusion.2
  590.0 4.4 pad_maximum_fusion.11
  594.4 4.1 convolution_add_fusion.1
  598.5 2.9 fusion.8
  601.4 3.4 copy.141
  604.8 5.5 reshape.210
  610.3 3.3 fusion.15
  (134 shorter events, 58.0 us)
Async XLA Ops:
  2.9 18.7 %all-to-all-start = ((s32[128,1,2]{2,1,0:T(1,128)}), s32[128,1,2]{2,1,0:T(1,128)S(1)}, u32[]{:S(2)}, u32[]{:S(2)}) async-start(s32[128,1,2]{2,1,0:T(1,128)} %bitcast), calls=%async_computation | async-start | bytes 131072 | tf_op jit(solution)/shard_map/all_to_all | solution.py:116
  21.6 14.1 %all-to-all-start.1 = ((bf16[128,2,128]{2,1,0:T(2,128)(2,1)}), bf16[128,2,128]{2,1,0:T(2,128)(2,1)S(1)}, u32[]{:S(2)}, u32[]{:S(2)}) async-start(bf16[128,2,128]{2,1,0:T(2,128)(2,1)} %bitcast.2), calls=%async_computation.1 | async-start | bytes 131072 | tf_op jit(solution)/shard_map/all_to_all | solution.py:109
  36.9 7.4 %collective-permute-start.1 = (bf16[2,1,2048]{2,1,0:T(2,128)(2,1)S(1)}, bf16[2,1,2048]{2,1,0:T(2,128)(2,1)S(1)}, u32[]{:S(2)}, u32[]{:S(2)}) collective-permute-start(bf16[2,1,2048]{2,1,0:T(2,128)(2,1)S(1)} %get-tuple-element.74), channel_id=1, source_target_pairs={{1,0},{2,1},{3,2},{4,3},{5,4},{6,5},{7,6},{8,7},{9,8},{10,9},{11,1... | collective-permute-start | bytes 24584 | tf_op jit(solution)/shard_map/ppermute | solution.py:22
  39.3 5.9 collective-permute-start
  45.2 5.7 collective-permute-start.2
  56.2 6.2 %copy-start.15 = (bf16[2,4,128,16]{3,2,0,1:T(8,128)(2,1)S(1)}, bf16[2,4,128,16]{3,2,0,1:T(8,128)(2,1)}, u32[]{:S(2)}) copy-start(bf16[2,4,128,16]{3,2,0,1:T(8,128)(2,1)} %get-tuple-element.54) | copy-start | bytes 98308
  56.2 6.2 %copy-start.16 = (bf16[2,4,128,16]{3,2,0,1:T(8,128)(2,1)S(1)}, bf16[2,4,128,16]{3,2,0,1:T(8,128)(2,1)}, u32[]{:S(2)}) copy-start(bf16[2,4,128,16]{3,2,0,1:T(8,128)(2,1)} %get-tuple-element.68) | copy-start | bytes 98308
  62.3 9.5 %copy-start.14 = (bf16[2,4,128,16]{3,2,0,1:T(8,128)(2,1)S(1)}, bf16[2,4,128,16]{3,2,0,1:T(8,128)(2,1)}, u32[]{:S(2)}) copy-start(bf16[2,4,128,16]{3,2,0,1:T(8,128)(2,1)} %get-tuple-element.50) | copy-start | bytes 98308
  71.8 9.6 %copy-start.12 = (bf16[2,4,128,16]{3,2,0,1:T(8,128)(2,1)S(1)}, bf16[2,4,128,16]{3,2,0,1:T(8,128)(2,1)}, u32[]{:S(2)}) copy-start(bf16[2,4,128,16]{3,2,0,1:T(8,128)(2,1)} %get-tuple-element.71) | copy-start | bytes 98308
  71.8 9.6 %copy-start.13 = (bf16[2,4,128,16]{3,2,0,1:T(8,128)(2,1)S(1)}, bf16[2,4,128,16]{3,2,0,1:T(8,128)(2,1)}, u32[]{:S(2)}) copy-start(bf16[2,4,128,16]{3,2,0,1:T(8,128)(2,1)} %get-tuple-element.72) | copy-start | bytes 98308
  81.4 6.0 copy-start.21
  92.5 3.2 copy-start.17
  94.1 1.7 copy-start.11
  95.8 13.2 %copy-start.19 = (f32[384]{0:T(512)S(1)}, f32[384]{0:T(512)}, u32[]{:S(2)}) copy-start(f32[384]{0:T(512)} %param.14) | copy-start | bytes 4612
  100.6 10.5 %collective-permute-start.4 = (bf16[2,1,49152]{2,0,1:T(2,128)(2,1)S(1)}, bf16[2,1,49152]{2,0,1:T(2,128)(2,1)S(1)}, u32[]{:S(2)}, u32[]{:S(2)}) collective-permute-start(bf16[2,1,49152]{2,0,1:T(2,128)(2,1)S(1)} %get-tuple-element.45), channel_id=1, source_target_pairs={{1,0},{2,1},{3,2},{4,3},{5,4},{6,5},{7,6},{8,7},{9,8},{10,9},{11,1... | collective-permute-start | bytes 589832 | tf_op jit(solution)/shard_map/ppermute | solution.py:22
  102.5 10.3 %collective-permute-start.3 = (bf16[2,1,49152]{2,0,1:T(2,128)(2,1)S(1)}, bf16[2,1,49152]{2,0,1:T(2,128)(2,1)S(1)}, u32[]{:S(2)}, u32[]{:S(2)}) collective-permute-start(bf16[2,1,49152]{2,0,1:T(2,128)(2,1)S(1)} %get-tuple-element.44), channel_id=1, source_target_pairs={{0,1},{1,2},{2,3},{3,4},{4,5},{5,6},{6,7},{7,8},{8,9},{9,10},{10,1... | collective-permute-start | bytes 589832 | tf_op jit(solution)/shard_map/ppermute | solution.py:19
  233.0 9.2 %copy-start.18 = (bf16[3456,192]{0,1:T(8,128)(2,1)S(1)}, bf16[3456,192]{0,1:T(8,128)(2,1)}, u32[]{:S(2)}) copy-start(bf16[3456,192]{0,1:T(8,128)(2,1)} %param.15) | copy-start | bytes 3981316
  242.3 14.2 %slice-start = ((s8[9437184]{0:T(1024)(128)(4,1)}), s8[4194304]{0:T(1024)(128)(4,1)S(1)}, s32[]{:S(2)}) async-start(s8[9437184]{0:T(1024)(128)(4,1)} %bitcast.120), calls=%async_computation.3 | async-start | bytes 8388608
  242.3 14.2 %slice-start.1 = ((s8[9437184]{0:T(1024)(128)(4,1)}), s8[4194304]{0:T(1024)(128)(4,1)S(1)}, s32[]{:S(2)}) async-start(s8[9437184]{0:T(1024)(128)(4,1)} %bitcast.120), calls=%async_computation.4 | async-start | bytes 8388608
  249.4 7.1 %slice-start.2 = ((s8[9437184]{0:T(1024)(128)(4,1)}), s8[1048576]{0:T(1024)(128)(4,1)S(1)}, s32[]{:S(2)}) async-start(s8[9437184]{0:T(1024)(128)(4,1)} %bitcast.120), calls=%async_computation.5 | async-start | bytes 2097152
  249.4 7.1 %copy-start.23 = (f32[192]{0:T(256)S(1)}, f32[192]{0:T(256)}, u32[]{:S(2)}) copy-start(f32[192]{0:T(256)} %param.16) | copy-start | bytes 2308
  445.4 3.3 copy-start.1
  448.7 3.4 copy-start
  448.7 3.5 copy-start.22
  453.7 6.3 %collective-permute-start.6 = (bf16[16,8,1,192]{3,2,1,0:T(2,128)(2,1)S(1)}, bf16[16,8,1,192]{3,2,1,0:T(2,128)(2,1)S(1)}, u32[]{:S(2)}, u32[]{:S(2)}) collective-permute-start(bf16[16,8,1,192]{3,2,1,0:T(2,128)(2,1)S(1)} %get-tuple-element.43), channel_id=1, source_target_pairs={{16,0},{32,16},{48,32},{64,48},{80,64},{96,80},{112,96},{17,1},{33... | collective-permute-start | bytes 147464 | tf_op jit(solution)/shard_map/ppermute | solution.py:22
  456.6 4.5 collective-permute-start.5
  461.5 14.3 %collective-permute-start.7 = (bf16[16,1,34,192]{3,2,1,0:T(8,128)(2,1)S(1)}, bf16[16,1,34,192]{3,2,1,0:T(8,128)(2,1)S(1)}, u32[]{:S(2)}, u32[]{:S(2)}) collective-permute-start(bf16[16,1,34,192]{3,2,1,0:T(8,128)(2,1)S(1)} %get-tuple-element.40), channel_id=1, source_target_pairs={{0,1},{1,2},{2,3},{3,4},{4,5},{5,6},{6,7},{7,8},{8,9},{9,10},{10,1... | collective-permute-start | bytes 626696 | tf_op jit(solution)/shard_map/ppermute | solution.py:19
  467.7 13.0 %collective-permute-start.8 = (bf16[16,1,34,192]{3,2,1,0:T(8,128)(2,1)S(1)}, bf16[16,1,34,192]{3,2,1,0:T(8,128)(2,1)S(1)}, u32[]{:S(2)}, u32[]{:S(2)}) collective-permute-start(bf16[16,1,34,192]{3,2,1,0:T(8,128)(2,1)S(1)} %get-tuple-element.41), channel_id=1, source_target_pairs={{1,0},{2,1},{3,2},{4,3},{5,4},{6,5},{7,6},{8,7},{9,8},{10,9},{11,1... | collective-permute-start | bytes 626696 | tf_op jit(solution)/shard_map/ppermute | solution.py:22
  515.7 6.2 %copy-start.9 = (bf16[16,8,32,192]{3,2,1,0:T(8,128)(2,1)S(1)}, bf16[16,8,32,192]{3,2,1,0:T(8,128)(2,1)}, u32[]{:S(2)}) copy-start(bf16[16,8,32,192]{3,2,1,0:T(8,128)(2,1)} %get-tuple-element.29) | copy-start | bytes 4718596
  534.2 4.3 copy-start.8
  542.9 6.0 copy-start.7
  553.3 5.8 copy-start.6
  563.6 5.8 copy-start.5
  573.8 5.8 copy-start.4
  584.2 5.8 copy-start.10
  594.4 4.1 copy-start.3
  594.4 4.1 copy-start.20
  604.8 5.5 copy-start.2
where the time goes:
time: 624 us; the launch traced here: 614 us
  local copies, waits for them, and re-layouts  272 us (44%)
  other arithmetic  153 us (25%)
  matrix products  88.2 us (14%)
  starting transfers between devices  50.7 us (8%)
  blocking collectives  24.8 us (4%)
  waiting for transfers between devices  23.7 us (4%)
    concatenate x3, other arithmetic, upsample_conv(): jnp.concatenate([doubled[:, row_off:row_off + height, col_off:col_off + b...  75 us
    dot_general x18, matrix products, causal_taps(): jnp.dot(window.reshape(-1, 3 * channels), weight[start:start + 3 * channe...  69.6 us
    unnamed x60, local copies, waits for them, and re-layouts  64 us
    concatenate x14, other arithmetic, causal_taps(): jnp.concatenate([padded[time_off:time_off + frames, row_off:row_off + hei...  54.5 us
    another operation x2, local copies, waits for them, and re-layouts, local(): section_out.reshape(FS, 2 * TH, 2 * W * C2)  47.3 us
    all_to_all x1, local copies, waits for them, and re-layouts, local(): lax.all_to_all(section_out.reshape(FS, 2 * TH, 2 * W * C2), 'seq', split_...  45.4 us
    concatenate x3, local copies, waits for them, and re-layouts, upsample_conv(): jnp.concatenate([doubled[:, row_off:row_off + height, col_off:col_off + b...  27.4 us
    slice x6, local copies, waits for them, and re-layouts, causal_taps(): padded[time_off:time_off + frames, row_off:row_off + height, col_off:col_...  27.3 us
  transfers between devices with their start and end apart: 11, of which 8 were waited for; matrix products, arithmetic and copies ran while one was open for 2% of the time, Pallas kernels for 0%

commit v1 on v0

--- a/solution.py
+++ b/solution.py
@@ -136,8 +136,16 @@
     act_ext = extended_2(first_act.reshape(FS, TH, W * C1), (("tile", 1),), 1)
     act_ext = jnp.pad(act_ext.reshape(FS, TH + 2, W, C1), ((0, 0), (0, 0), (1, 1), (0, 0)))
     section_out = upsample_conv(act_ext, w_up, b_up)
-    upsampled = lax.all_to_all(
-        section_out.reshape(FS, 2 * TH, 2 * W * C2), "seq", split_axis=2, concat_axis=0, tiled=True
+    upsampled = jnp.concatenate(
+        lax.all_to_all(
+            jnp.stack(
+                jnp.split(section_out.reshape(FS, 2 * TH, 2 * W * C2), lax.axis_size("seq"), axis=2)
+            ),
+            "seq",
+            0,
+            0,
+        ),
+        axis=0,
     )
     upsampled = upsampled.reshape(FS * seq_count, 2 * TH, 2 * W // seq_count, C2)
     res_act = normed_silu(upsampled.astype(jnp.float32), gain_res)

time: 624 us -> 473 us (0.76)
  local copies, waits for them, and re-layouts: 272 us -> 127 us
    unnamed x60 -> x64, local copies, waits for them, and re-layouts: 64 us -> 8.51 us
    all_to_all x1 -> x0, local copies, waits for them, and re-layouts: 45.4 us -> none  [local(): lax.all_to_all(section_out.reshape(FS, 2 * TH, 2 * W * C2), 'seq', split_...]
    another operation x2 -> x1, local copies, waits for them, and re-layouts: 47.3 us -> 3.19 us  [local(): section_out.reshape(FS, 2 * TH, 2 * W * C2)]
where the time goes in v1:
time: 473 us; the launch traced here: 468 us
  other arithmetic  153 us (32%)
  local copies, waits for them, and re-layouts  127 us (27%)
  matrix products  87.9 us (19%)
  starting transfers between devices  50.7 us (11%)
  blocking collectives  24.6 us (5%)
  waiting for transfers between devices  24 us (5%)
    concatenate x3, other arithmetic, upsample_conv(): jnp.concatenate([doubled[:, row_off:row_off + height, col_off:col_off + b...  75 us
    dot_general x18, matrix products, causal_taps(): jnp.dot(window.reshape(-1, 3 * channels), weight[start:start + 3 * channe...  69.3 us
    concatenate x14, other arithmetic, causal_taps(): jnp.concatenate([padded[time_off:time_off + frames, row_off:row_off + hei...  54.5 us
    concatenate x3, local copies, waits for them, and re-layouts, upsample_conv(): jnp.concatenate([doubled[:, row_off:row_off + height, col_off:col_off + b...  27.4 us
    slice x6, local copies, waits for them, and re-layouts, causal_taps(): padded[time_off:time_off + frames, row_off:row_off + height, col_off:col_...  27.2 us
    all_to_all x1, blocking collectives, local(): lax.all_to_all(jnp.stack(jnp.split(section_out.reshape(FS, 2 * TH, 2 * W...  24.6 us
    slice x1, local copies, waits for them, and re-layouts, upsample_conv(): doubled[:, row_off:row_off + height, col_off:col_off + breadth]  20.7 us
    ppermute x4, starting transfers between devices, extended_2(): lax.ppermute(lax.slice_in_dim(block, block.shape[dim] - width, None, axis...  20.1 us
  transfers between devices with their start and end apart: 11, of which 8 were waited for; matrix products, arithmetic and copies ran while one was open for 2% of the time, Pallas kernels for 0%

profile of v1, /device:TPU:7, one launch (start us, length us, event | category | flops | bytes accessed | tf_op | source)
XLA Modules:
  0.0 468.3 jit_solution(2319685513492756941)
XLA Ops:
  2.9 10.8 %all-to-all-start = ((s32[128,1,2]{2,1,0:T(1,128)}), s32[128,1,2]{2,1,0:T(1,128)S(1)}, u32[]{:S(2)}, u32[]{:S(2)}) async-start(s32[128,1,2]{2,1,0:T(1,128)} %bitcast), calls=%async_computation | async-start | bytes 131072 | tf_op jit(solution)/shard_map/all_to_all | solution.py:116
  15.4 6.2 %all-to-all-done = s32[128,1,2]{2,1,0:T(1,128)S(1)} async-done(((s32[128,1,2]{2,1,0:T(1,128)}), s32[128,1,2]{2,1,0:T(1,128)S(1)}, u32[]{:S(2)}, u32[]{:S(2)}) %all-to-all-start) | async-done | bytes 1056 | tf_op jit(solution)/shard_map/all_to_all | solution.py:116
  21.6 6.1 %all-to-all-start.1 = ((bf16[128,2,128]{2,1,0:T(2,128)(2,1)}), bf16[128,2,128]{2,1,0:T(2,128)(2,1)S(1)}, u32[]{:S(2)}, u32[]{:S(2)}) async-start(bf16[128,2,128]{2,1,0:T(2,128)(2,1)} %bitcast.2), calls=%async_computation.1 | async-start | bytes 131072 | tf_op jit(solution)/shard_map/all_to_all | solution.py:109
  29.1 6.5 %all-to-all-done.1 = bf16[128,2,128]{2,1,0:T(2,128)(2,1)S(1)} async-done(((bf16[128,2,128]{2,1,0:T(2,128)(2,1)}), bf16[128,2,128]{2,1,0:T(2,128)(2,1)S(1)}, u32[]{:S(2)}, u32[]{:S(2)}) %all-to-all-start.1) | async-done | bytes 65568 | tf_op jit(solution)/shard_map/all_to_all | solution.py:109
  36.9 2.4 collective-permute-start.1
  39.3 5.0 %collective-permute-start = (bf16[2,1,2048]{2,1,0:T(2,128)(2,1)S(1)}, bf16[2,1,2048]{2,1,0:T(2,128)(2,1)S(1)}, u32[]{:S(2)}, u32[]{:S(2)}) collective-permute-start(bf16[2,1,2048]{2,1,0:T(2,128)(2,1)S(1)} %get-tuple-element.73), channel_id=1, source_target_pairs={{0,1},{1,2},{2,3},{3,4},{4,5},{5,6},{6,7},{7,8},{8,9},{9,10},{10,1... | collective-permute-start | bytes 24584 | tf_op jit(solution)/shard_map/ppermute | solution.py:19
  45.2 4.6 collective-permute-start.2
  60.3 2.3 fusion.45
  62.6 2.5 pad_maximum_fusion.22
  66.3 2.4 fusion.47
  69.8 2.3 fusion.49
  72.1 2.6 pad_maximum_fusion.20
  75.9 2.3 fusion.51
  79.4 2.4 fusion.53
  84.1 2.3 fusion.57
  87.8 4.8 %multiply_reduce_fusion.1 = (f32[1024]{0:T(1024)S(1)}, f32[1024,384]{1,0:T(8,128)S(1)}) fusion(f32[384]{0:T(512)S(1)} %copy-done.21, bf16[1024,48]{0,1:T(8,128)(2,1)S(1)} %reshape.187, bf16[432,384]{1,0:T(8,128)(2,1)} %param.12, f32[1024,384]{1,0:T(8,128)S(1)} %fusion.43, f32[1024,384]{1,0:T(8,128)} %fusion.45, f32[1024,384]{1,0:T(8,128)} %fusion.47, ...), kind=kOutput, calls=%fused_computation.51 | convolution fusion | flops 42073088 | bytes 14296576 | tf_op jit(solution)/shard_map/dot_general | solution.py:53
  96.1 4.5 fusion.17
  102.8 6.2 %collective-permute-start.3 = (bf16[2,1,49152]{2,0,1:T(2,128)(2,1)S(1)}, bf16[2,1,49152]{2,0,1:T(2,128)(2,1)S(1)}, u32[]{:S(2)}, u32[]{:S(2)}) collective-permute-start(bf16[2,1,49152]{2,0,1:T(2,128)(2,1)S(1)} %get-tuple-element.44), channel_id=1, source_target_pairs={{0,1},{1,2},{2,3},{3,4},{4,5},{5,6},{6,7},{7,8},{8,9},{9,10},{10,1... | collective-permute-start | bytes 589832 | tf_op jit(solution)/shard_map/ppermute | solution.py:19
  116.8 2.7 broadcast_in_dim.14
  119.5 20.7 %fusion.65 = (bf16[2,8,256,384]{3,0,2,1:T(2,128)(2,1)S(1)}, bf16[2,8,256,384]{3,0,2,1:T(2,128)(2,1)}, bf16[2,8,256,384]{3,0,2,1:T(2,128)(2,1)}, bf16[2,8,256,384...) fusion(bf16[2,12,260,384]{3,0,2,1:T(2,128)(2,1)S(1)} %bitcast.123), kind=kLoop, calls=%fused_computation.155 | loop fusion | bytes 56623104 | tf_op jit(solution)/shard_map/slice | solution.py:71
  140.2 30.7 %pad_maximum_fusion = bf16[2,8,256,1152]{3,0,2,1:T(2,128)(2,1)} fusion(bf16[2,8,256,384]{3,0,2,1:T(2,128)(2,1)S(1)} %get-tuple-element.11, bf16[2,8,256,384]{3,0,2,1:T(2,128)(2,1)S(1)} %get-tuple-element.12, bf16[2,8,256,384]{3,0,2,1:T(2,128)(2,1)S(1)} %get-tuple-element.13), kind=kLoop, calls=%fused_computation.3 | loop fusion | flops 28311552 | bytes 18874368 | tf_op jit(solution)/shard_map/concatenate | solution.py:69
  170.9 9.1 %copy.102 = bf16[2,8,256,1152]{3,2,1,0:T(8,128)(2,1)} copy(bf16[2,8,256,1152]{3,0,2,1:T(2,128)(2,1)} %pad_maximum_fusion) | data formatting | bytes 18874368 | tf_op jit(solution)/shard_map/concatenate | solution.py:69
  180.0 13.1 %pad_maximum_fusion.1 = bf16[2,8,256,1152]{3,0,2,1:T(2,128)(2,1)} fusion(bf16[2,8,256,384]{3,0,2,1:T(2,128)(2,1)} %get-tuple-element.8, bf16[2,8,256,384]{3,0,2,1:T(2,128)(2,1)} %get-tuple-element.9, bf16[2,8,256,384]{3,0,2,1:T(2,128)(2,1)} %get-tuple-element.10), kind=kLoop, calls=%fused_computation.4 | loop fusion | flops 28311552 | bytes 18874368 | tf_op jit(solution)/shard_map/concatenate | solution.py:69
  193.0 9.1 %copy.103 = bf16[2,8,256,1152]{3,2,1,0:T(8,128)(2,1)} copy(bf16[2,8,256,1152]{3,0,2,1:T(2,128)(2,1)} %pad_maximum_fusion.1) | data formatting | bytes 18874368 | tf_op jit(solution)/shard_map/concatenate | solution.py:69
  202.1 31.3 %pad_maximum_fusion.2 = bf16[2,8,256,1152]{3,0,2,1:T(2,128)(2,1)} fusion(bf16[2,8,256,384]{3,0,2,1:T(2,128)(2,1)} %get-tuple-element.6, bf16[2,8,256,384]{3,0,2,1:T(2,128)(2,1)} %get-tuple-element.7, bf16[2,8,256,384]{3,0,2,1:T(2,128)(2,1)S(1)} %get-tuple-element.5), kind=kLoop, calls=%fused_computation.5 | loop fusion | flops 28311552 | bytes 18874368 | tf_op jit(solution)/shard_map/concatenate | solution.py:69
  233.4 9.2 %copy.104 = bf16[2,8,256,1152]{3,2,1,0:T(8,128)(2,1)} copy(bf16[2,8,256,1152]{3,0,2,1:T(2,128)(2,1)} %pad_maximum_fusion.2) | data formatting | bytes 18874368 | tf_op jit(solution)/shard_map/concatenate | solution.py:69
  242.6 7.1 %fusion.20 = f32[4096,192]{0,1:T(8,128)S(1)} fusion(bf16[4096,1152]{1,0:T(8,128)(2,1)} %bitcast.136, bf16[3456,192]{0,1:T(8,128)(2,1)S(1)} %copy-done.18), kind=kOutput, calls=%fused_computation.57 | convolution fusion | flops 1811939328 | bytes 13025280 | tf_op jit(solution)/shard_map/dot_general | solution.py:77
  249.7 7.1 %convolution_add_fusion.8 = f32[4096,192]{0,1:T(8,128)S(1)} fusion(f32[4096,192]{0,1:T(8,128)S(1)} %fusion.20, bf16[4096,1152]{1,0:T(8,128)(2,1)} %bitcast.124, bf16[3456,192]{0,1:T(8,128)(2,1)S(1)} %copy-done.18), kind=kOutput, calls=%fused_computation.35 | convolution fusion | flops 1812725760 | bytes 16171008 | tf_op jit(solution)/shard_map/dot_general | solution.py:77
  256.9 4.4 fusion.10
  261.3 3.1 copy.105
  264.5 3.2 reshape_reshape.4
  275.2 24.6 %all_to_all.19 = bf16[8,2,8,6144]{3,2,1,0:T(8,128)(2,1)S(1)} all-to-all(bf16[8,2,8,6144]{3,2,1,0:T(8,128)(2,1)S(1)} %fusion.33), channel_id=1, replica_groups=mesh['seq'=8,'tile'=16] {'seq'}, dimensions={0} | all-to-all | bytes 3145728 | tf_op jit(solution)/shard_map/all_to_all | solution.py:140
  299.8 3.5 reshape.206
  303.3 3.0 multiply_reduce_fusion
  308.2 2.9 collective-permute-start.6
  311.2 2.6 collective-permute-start.5
  316.1 6.2 %collective-permute-start.7 = (bf16[16,1,34,192]{3,2,1,0:T(8,128)(2,1)S(1)}, bf16[16,1,34,192]{3,2,1,0:T(8,128)(2,1)S(1)}, u32[]{:S(2)}, u32[]{:S(2)}) collective-permute-start(bf16[16,1,34,192]{3,2,1,0:T(8,128)(2,1)S(1)} %get-tuple-element.40), channel_id=1, source_target_pairs={{0,1},{1,2},{2,3},{3,4},{4,5},{5,6},{6,7},{7,8},{8,9},{9,10},{10,1... | collective-permute-start | bytes 626696 | tf_op jit(solution)/shard_map/ppermute | solution.py:19
  324.2 6.1 %fusion.5 = bf16[16,8,32,576]{3,2,1,0:T(8,128)(2,1)S(1)} fusion(bf16[16,8,1,192]{3,2,1,0:T(2,128)(2,1)S(1)} %collective-permute-done.6, bf16[16,8,32,192]{3,2,1,0:T(8,128)(2,1)S(1)} %multiply_convert_fusion, bf16[16,8,1,192]{3,2,1,0:T(2,128)(2,1)S(1)} %collective-permute-done.5), kind=kLoop, calls=%fused_computation.13 | loop fusion | flops 23592960 | bytes 6389760 | tf_op jit(solution)/shard_map/concatenate | solution.py:41
  330.4 5.0 %collective-permute-done.8 = bf16[16,1,34,192]{3,2,1,0:T(8,128)(2,1)S(1)} collective-permute-done((bf16[16,1,34,192]{3,2,1,0:T(8,128)(2,1)S(1)}, bf16[16,1,34,192]{3,2,1,0:T(8,128)(2,1)S(1)}, u32[]{:S(2)}, u32[]{:S(2)}) %collective-permute-start.8) | collective-permute-done | bytes 208928 | tf_op jit(solution)/shard_map/ppermute | solution.py:22
  335.3 4.9 %maximum_maximum_fusion = (bf16[16,9,34,192]{3,2,1,0:T(8,128)(2,1)S(1)}, bf16[16,9,34,192]{3,2,1,0:T(8,128)(2,1)S(1)}) fusion(bf16[16,8,1,192]{3,2,1,0:T(2,128)(2,1)S(1)} %collective-permute-done.6, bf16[16,8,32,192]{3,2,1,0:T(8,128)(2,1)S(1)} %multiply_convert_fusion, bf16[16,8,1,192]{3,2,1,0:T(2,128)(2,1)S(1)} %collective-permute-done.5, ...), kind=kLoop, calls=%fused_computation.45 | loop fusion | flops 15040512 | bytes 5849088 | tf_op jit(solution)/shard_map/concatenate | solution.py:23
  340.3 4.2 fusion.68
  344.5 3.7 fusion.12
  348.2 14.8 %fusion.66 = (bf16[16,8,32,192]{3,2,1,0:T(8,128)(2,1)}, bf16[16,8,32,192]{3,2,1,0:T(8,128)(2,1)}, bf16[16,8,32,192]{3,2,1,0:T(8,128)(2,1)}, bf16[16,8,32,192]{3,...) fusion(bf16[18,10,34,192]{3,2,1,0:T(8,128)(2,1)S(1)} %fusion.12), kind=kLoop, calls=%fused_computation.156 | loop fusion | bytes 56623104 | tf_op jit(solution)/shard_map/slice | solution.py:43
  362.9 7.3 %pad_maximum_fusion.12 = bf16[16,8,32,576]{3,2,1,0:T(8,128)(2,1)} fusion(bf16[16,8,32,192]{3,2,1,0:T(8,128)(2,1)} %get-tuple-element.36, bf16[16,8,32,192]{3,2,1,0:T(8,128)(2,1)} %get-tuple-element.37, bf16[16,8,32,192]{3,2,1,0:T(8,128)(2,1)} %get-tuple-element.35), kind=kLoop, calls=%fused_computation.23 | loop fusion | flops 14155776 | bytes 9437184 | tf_op jit(solution)/shard_map/concatenate | solution.py:41
  370.3 6.3 %fusion.22 = f32[4096,192]{0,1:T(8,128)} fusion(bf16[4096,576]{1,0:T(8,128)(2,1)} %bitcast.132, bf16[5184,192]{0,1:T(8,128)(2,1)} %param.18), kind=kOutput, calls=%fused_computation.71 | convolution fusion | flops 905969664 | bytes 8634368 | tf_op jit(solution)/shard_map/dot_general | solution.py:53
  376.6 6.1 %pad_maximum_fusion.5 = bf16[16,8,32,576]{3,2,1,0:T(8,128)(2,1)} fusion(bf16[16,8,32,192]{3,2,1,0:T(8,128)(2,1)S(1)} %get-tuple-element.28, bf16[16,8,32,192]{3,2,1,0:T(8,128)(2,1)S(1)} %copy-done.9, bf16[16,8,32,192]{3,2,1,0:T(8,128)(2,1)} %get-tuple-element.30), kind=kLoop, calls=%fused_computation.16 | loop fusion | flops 14155776 | bytes 9437184 | tf_op jit(solution)/shard_map/concatenate | solution.py:41
  382.7 6.0 %fusion.31 = f32[4096,192]{0,1:T(8,128)} fusion(bf16[4096,576]{1,0:T(8,128)(2,1)} %bitcast.133, bf16[5184,192]{0,1:T(8,128)(2,1)} %param.18), kind=kOutput, calls=%fused_computation.80 | convolution fusion | flops 905969664 | bytes 8634368 | tf_op jit(solution)/shard_map/dot_general | solution.py:53
  388.8 4.2 fusion.67
  393.0 4.5 pad_maximum_fusion.6
  397.5 5.9 %convolution_add_fusion.6 = f32[4096,192]{0,1:T(8,128)} fusion(f32[4096,192]{0,1:T(8,128)} %fusion.31, bf16[4096,576]{1,0:T(8,128)(2,1)S(1)} %bitcast.126, bf16[5184,192]{0,1:T(8,128)(2,1)} %param.18), kind=kOutput, calls=%fused_computation.30 | convolution fusion | flops 906756096 | bytes 11255808 | tf_op jit(solution)/shard_map/dot_general | solution.py:53
  403.4 4.5 pad_maximum_fusion.7
  407.8 5.7 %convolution_add_fusion.5 = f32[4096,192]{0,1:T(8,128)} fusion(f32[4096,192]{0,1:T(8,128)} %convolution_add_fusion.6, bf16[4096,576]{1,0:T(8,128)(2,1)S(1)} %bitcast.127, bf16[5184,192]{0,1:T(8,128)(2,1)} %param.18), kind=kOutput, calls=%fused_computation.29 | convolution fusion | flops 906756096 | bytes 11255808 | tf_op jit(solution)/shard_map/dot_general | solution.py:53
  413.6 4.5 pad_maximum_fusion.8
  418.0 5.7 %convolution_add_fusion.4 = f32[4096,192]{0,1:T(8,128)} fusion(f32[4096,192]{0,1:T(8,128)} %convolution_add_fusion.5, bf16[4096,576]{1,0:T(8,128)(2,1)S(1)} %bitcast.128, bf16[5184,192]{0,1:T(8,128)(2,1)} %param.18), kind=kOutput, calls=%fused_computation.28 | convolution fusion | flops 906756096 | bytes 11255808 | tf_op jit(solution)/shard_map/dot_general | solution.py:53
  423.7 4.5 pad_maximum_fusion.9
  428.2 5.7 %convolution_add_fusion.3 = f32[4096,192]{0,1:T(8,128)} fusion(f32[4096,192]{0,1:T(8,128)} %convolution_add_fusion.4, bf16[4096,576]{1,0:T(8,128)(2,1)S(1)} %bitcast.129, bf16[5184,192]{0,1:T(8,128)(2,1)} %param.18), kind=kOutput, calls=%fused_computation.27 | convolution fusion | flops 906756096 | bytes 11255808 | tf_op jit(solution)/shard_map/dot_general | solution.py:53
  433.9 4.6 pad_maximum_fusion.10
  438.6 5.7 %convolution_add_fusion.2 = f32[4096,192]{0,1:T(8,128)} fusion(f32[4096,192]{0,1:T(8,128)} %convolution_add_fusion.3, bf16[4096,576]{1,0:T(8,128)(2,1)S(1)} %bitcast.130, bf16[5184,192]{0,1:T(8,128)(2,1)} %param.18), kind=kOutput, calls=%fused_computation.26 | convolution fusion | flops 906756096 | bytes 11255808 | tf_op jit(solution)/shard_map/dot_general | solution.py:53
  444.3 4.4 pad_maximum_fusion.11
  448.7 4.1 convolution_add_fusion.1
  452.8 2.9 fusion.8
  455.7 3.4 copy.106
  459.1 5.5 %reshape.204 = f32[16,8,6144]{2,1,0:T(8,128)} reshape(f32[4096,192]{1,0:T(8,128)} %copy.106) | data formatting | bytes 6291456 | tf_op jit(solution)/shard_map/reshape | solution.py:58
  464.6 3.3 fusion.15
  (136 shorter events, 53.9 us)
Async XLA Ops:
  2.9 18.7 %all-to-all-start = ((s32[128,1,2]{2,1,0:T(1,128)}), s32[128,1,2]{2,1,0:T(1,128)S(1)}, u32[]{:S(2)}, u32[]{:S(2)}) async-start(s32[128,1,2]{2,1,0:T(1,128)} %bitcast), calls=%async_computation | async-start | bytes 131072 | tf_op jit(solution)/shard_map/all_to_all | solution.py:116
  21.6 14.1 %all-to-all-start.1 = ((bf16[128,2,128]{2,1,0:T(2,128)(2,1)}), bf16[128,2,128]{2,1,0:T(2,128)(2,1)S(1)}, u32[]{:S(2)}, u32[]{:S(2)}) async-start(bf16[128,2,128]{2,1,0:T(2,128)(2,1)} %bitcast.2), calls=%async_computation.1 | async-start | bytes 131072 | tf_op jit(solution)/shard_map/all_to_all | solution.py:109
  36.9 7.4 %collective-permute-start.1 = (bf16[2,1,2048]{2,1,0:T(2,128)(2,1)S(1)}, bf16[2,1,2048]{2,1,0:T(2,128)(2,1)S(1)}, u32[]{:S(2)}, u32[]{:S(2)}) collective-permute-start(bf16[2,1,2048]{2,1,0:T(2,128)(2,1)S(1)} %get-tuple-element.74), channel_id=1, source_target_pairs={{1,0},{2,1},{3,2},{4,3},{5,4},{6,5},{7,6},{8,7},{9,8},{10,9},{11,1... | collective-permute-start | bytes 24584 | tf_op jit(solution)/shard_map/ppermute | solution.py:22
  39.3 5.9 %collective-permute-start = (bf16[2,1,2048]{2,1,0:T(2,128)(2,1)S(1)}, bf16[2,1,2048]{2,1,0:T(2,128)(2,1)S(1)}, u32[]{:S(2)}, u32[]{:S(2)}) collective-permute-start(bf16[2,1,2048]{2,1,0:T(2,128)(2,1)S(1)} %get-tuple-element.73), channel_id=1, source_target_pairs={{0,1},{1,2},{2,3},{3,4},{4,5},{5,6},{6,7},{7,8},{8,9},{9,10},{10,1... | collective-permute-start | bytes 24584 | tf_op jit(solution)/shard_map/ppermute | solution.py:19
  45.2 6.0 %collective-permute-start.2 = (bf16[2,6,2048]{2,1,0:T(8,128)(2,1)S(1)}, bf16[2,6,2048]{2,1,0:T(8,128)(2,1)S(1)}, u32[]{:S(2)}, u32[]{:S(2)}) collective-permute-start(bf16[2,6,2048]{2,1,0:T(8,128)(2,1)S(1)} %pad_maximum_fusion.27), channel_id=1, source_target_pairs={{0,16},{16,32},{32,48},{48,64},{64,80},{80,96},{96,112},{1,17},{17... | collective-permute-start | bytes 147464 | tf_op jit(solution)/shard_map/ppermute | solution.py:30
  56.5 6.2 %copy-start.15 = (bf16[2,4,128,16]{3,2,0,1:T(8,128)(2,1)S(1)}, bf16[2,4,128,16]{3,2,0,1:T(8,128)(2,1)}, u32[]{:S(2)}) copy-start(bf16[2,4,128,16]{3,2,0,1:T(8,128)(2,1)} %get-tuple-element.54) | copy-start | bytes 98308
  56.5 6.2 %copy-start.16 = (bf16[2,4,128,16]{3,2,0,1:T(8,128)(2,1)S(1)}, bf16[2,4,128,16]{3,2,0,1:T(8,128)(2,1)}, u32[]{:S(2)}) copy-start(bf16[2,4,128,16]{3,2,0,1:T(8,128)(2,1)} %get-tuple-element.68) | copy-start | bytes 98308
  62.6 9.5 %copy-start.14 = (bf16[2,4,128,16]{3,2,0,1:T(8,128)(2,1)S(1)}, bf16[2,4,128,16]{3,2,0,1:T(8,128)(2,1)}, u32[]{:S(2)}) copy-start(bf16[2,4,128,16]{3,2,0,1:T(8,128)(2,1)} %get-tuple-element.50) | copy-start | bytes 98308
  72.1 9.6 %copy-start.12 = (bf16[2,4,128,16]{3,2,0,1:T(8,128)(2,1)S(1)}, bf16[2,4,128,16]{3,2,0,1:T(8,128)(2,1)}, u32[]{:S(2)}) copy-start(bf16[2,4,128,16]{3,2,0,1:T(8,128)(2,1)} %get-tuple-element.71) | copy-start | bytes 98308
  72.1 9.6 %copy-start.13 = (bf16[2,4,128,16]{3,2,0,1:T(8,128)(2,1)S(1)}, bf16[2,4,128,16]{3,2,0,1:T(8,128)(2,1)}, u32[]{:S(2)}) copy-start(bf16[2,4,128,16]{3,2,0,1:T(8,128)(2,1)} %get-tuple-element.72) | copy-start | bytes 98308
  81.7 6.0 %copy-start.21 = (f32[384]{0:T(512)S(1)}, f32[384]{0:T(512)}, u32[]{:S(2)}) copy-start(f32[384]{0:T(512)} %param.13) | copy-start | bytes 4612
  92.8 3.2 copy-start.17
  94.4 1.7 copy-start.11
  96.1 12.9 %copy-start.19 = (f32[384]{0:T(512)S(1)}, f32[384]{0:T(512)}, u32[]{:S(2)}) copy-start(f32[384]{0:T(512)} %param.14) | copy-start | bytes 4612
  100.9 10.5 %collective-permute-start.4 = (bf16[2,1,49152]{2,0,1:T(2,128)(2,1)S(1)}, bf16[2,1,49152]{2,0,1:T(2,128)(2,1)S(1)}, u32[]{:S(2)}, u32[]{:S(2)}) collective-permute-start(bf16[2,1,49152]{2,0,1:T(2,128)(2,1)S(1)} %get-tuple-element.45), channel_id=1, source_target_pairs={{1,0},{2,1},{3,2},{4,3},{5,4},{6,5},{7,6},{8,7},{9,8},{10,9},{11,1... | collective-permute-start | bytes 589832 | tf_op jit(solution)/shard_map/ppermute | solution.py:22
  102.8 10.3 %collective-permute-start.3 = (bf16[2,1,49152]{2,0,1:T(2,128)(2,1)S(1)}, bf16[2,1,49152]{2,0,1:T(2,128)(2,1)S(1)}, u32[]{:S(2)}, u32[]{:S(2)}) collective-permute-start(bf16[2,1,49152]{2,0,1:T(2,128)(2,1)S(1)} %get-tuple-element.44), channel_id=1, source_target_pairs={{0,1},{1,2},{2,3},{3,4},{4,5},{5,6},{6,7},{7,8},{8,9},{9,10},{10,1... | collective-permute-start | bytes 589832 | tf_op jit(solution)/shard_map/ppermute | solution.py:19
  233.4 9.2 %copy-start.18 = (bf16[3456,192]{0,1:T(8,128)(2,1)S(1)}, bf16[3456,192]{0,1:T(8,128)(2,1)}, u32[]{:S(2)}) copy-start(bf16[3456,192]{0,1:T(8,128)(2,1)} %param.15) | copy-start | bytes 3981316
  242.6 14.2 %slice-start = ((s8[9437184]{0:T(1024)(128)(4,1)}), s8[4194304]{0:T(1024)(128)(4,1)S(1)}, s32[]{:S(2)}) async-start(s8[9437184]{0:T(1024)(128)(4,1)} %bitcast.137), calls=%async_computation.3 | async-start | bytes 8388608
  242.6 14.2 %slice-start.1 = ((s8[9437184]{0:T(1024)(128)(4,1)}), s8[4194304]{0:T(1024)(128)(4,1)S(1)}, s32[]{:S(2)}) async-start(s8[9437184]{0:T(1024)(128)(4,1)} %bitcast.137), calls=%async_computation.4 | async-start | bytes 8388608
  249.7 7.1 %slice-start.2 = ((s8[9437184]{0:T(1024)(128)(4,1)}), s8[1048576]{0:T(1024)(128)(4,1)S(1)}, s32[]{:S(2)}) async-start(s8[9437184]{0:T(1024)(128)(4,1)} %bitcast.137), calls=%async_computation.5 | async-start | bytes 2097152
  249.7 7.1 %copy-start.23 = (f32[192]{0:T(256)S(1)}, f32[192]{0:T(256)}, u32[]{:S(2)}) copy-start(f32[192]{0:T(256)} %param.16) | copy-start | bytes 2308
  299.8 6.5 %copy-start.2 = (bf16[8,2,8,6144]{3,2,1,0:T(8,128)(2,1)}, bf16[8,2,8,6144]{3,2,1,0:T(8,128)(2,1)S(1)}, u32[]{:S(2)}) copy-start(bf16[8,2,8,6144]{3,2,1,0:T(8,128)(2,1)S(1)} %all_to_all.19) | copy-start | bytes 4718596
  303.3 3.4 copy-start
  303.3 3.4 copy-start.22
  308.2 6.3 %collective-permute-start.6 = (bf16[16,8,1,192]{3,2,1,0:T(2,128)(2,1)S(1)}, bf16[16,8,1,192]{3,2,1,0:T(2,128)(2,1)S(1)}, u32[]{:S(2)}, u32[]{:S(2)}) collective-permute-start(bf16[16,8,1,192]{3,2,1,0:T(2,128)(2,1)S(1)} %get-tuple-element.43), channel_id=1, source_target_pairs={{16,0},{32,16},{48,32},{64,48},{80,64},{96,80},{112,96},{17,1},{33... | collective-permute-start | bytes 147464 | tf_op jit(solution)/shard_map/ppermute | solution.py:22
  311.2 4.5 collective-permute-start.5
  316.1 14.3 %collective-permute-start.7 = (bf16[16,1,34,192]{3,2,1,0:T(8,128)(2,1)S(1)}, bf16[16,1,34,192]{3,2,1,0:T(8,128)(2,1)S(1)}, u32[]{:S(2)}, u32[]{:S(2)}) collective-permute-start(bf16[16,1,34,192]{3,2,1,0:T(8,128)(2,1)S(1)} %get-tuple-element.40), channel_id=1, source_target_pairs={{0,1},{1,2},{2,3},{3,4},{4,5},{5,6},{6,7},{7,8},{8,9},{9,10},{10,1... | collective-permute-start | bytes 626696 | tf_op jit(solution)/shard_map/ppermute | solution.py:19
  322.3 13.0 %collective-permute-start.8 = (bf16[16,1,34,192]{3,2,1,0:T(8,128)(2,1)S(1)}, bf16[16,1,34,192]{3,2,1,0:T(8,128)(2,1)S(1)}, u32[]{:S(2)}, u32[]{:S(2)}) collective-permute-start(bf16[16,1,34,192]{3,2,1,0:T(8,128)(2,1)S(1)} %get-tuple-element.41), channel_id=1, source_target_pairs={{1,0},{2,1},{3,2},{4,3},{5,4},{6,5},{7,6},{8,7},{9,8},{10,9},{11,1... | collective-permute-start | bytes 626696 | tf_op jit(solution)/shard_map/ppermute | solution.py:22
  370.3 6.3 %copy-start.9 = (bf16[16,8,32,192]{3,2,1,0:T(8,128)(2,1)S(1)}, bf16[16,8,32,192]{3,2,1,0:T(8,128)(2,1)}, u32[]{:S(2)}) copy-start(bf16[16,8,32,192]{3,2,1,0:T(8,128)(2,1)} %get-tuple-element.29) | copy-start | bytes 4718596
  388.8 4.2 copy-start.8
  397.5 5.9 %copy-start.7 = (bf16[16,8,32,192]{3,2,1,0:T(8,128)(2,1)S(1)}, bf16[16,8,32,192]{3,2,1,0:T(8,128)(2,1)}, u32[]{:S(2)}) copy-start(bf16[16,8,32,192]{3,2,1,0:T(8,128)(2,1)} %get-tuple-element.22) | copy-start | bytes 4718596
  407.8 5.7 %copy-start.6 = (bf16[16,8,32,192]{3,2,1,0:T(8,128)(2,1)S(1)}, bf16[16,8,32,192]{3,2,1,0:T(8,128)(2,1)}, u32[]{:S(2)}) copy-start(bf16[16,8,32,192]{3,2,1,0:T(8,128)(2,1)} %get-tuple-element.19) | copy-start | bytes 4718596
  418.0 5.7 %copy-start.5 = (bf16[16,8,32,192]{3,2,1,0:T(8,128)(2,1)S(1)}, bf16[16,8,32,192]{3,2,1,0:T(8,128)(2,1)}, u32[]{:S(2)}) copy-start(bf16[16,8,32,192]{3,2,1,0:T(8,128)(2,1)} %get-tuple-element.16) | copy-start | bytes 4718596
  428.2 5.7 %copy-start.4 = (bf16[16,8,32,192]{3,2,1,0:T(8,128)(2,1)S(1)}, bf16[16,8,32,192]{3,2,1,0:T(8,128)(2,1)}, u32[]{:S(2)}) copy-start(bf16[16,8,32,192]{3,2,1,0:T(8,128)(2,1)} %get-tuple-element.14) | copy-start | bytes 4718596
  438.6 5.7 %copy-start.10 = (bf16[16,8,32,192]{3,2,1,0:T(8,128)(2,1)S(1)}, bf16[16,8,32,192]{3,2,1,0:T(8,128)(2,1)}, u32[]{:S(2)}) copy-start(bf16[16,8,32,192]{3,2,1,0:T(8,128)(2,1)} %get-tuple-element.32) | copy-start | bytes 4718596
  448.6 4.1 copy-start.1
  448.7 4.1 copy-start.20
  459.1 5.5 %copy-start.3 = (bf16[8,2,8,6144]{3,2,1,0:T(8,128)(2,1)S(1)}, bf16[8,2,8,6144]{3,2,1,0:T(8,128)(2,1)}, u32[]{:S(2)}) copy-start(bf16[8,2,8,6144]{3,2,1,0:T(8,128)(2,1)} %copy-done.2) | copy-start | bytes 4718596
